TPU v7x, 256 devices: a whole 4x4x8 slice. The times are simulated.
256 devices in a mesh: chan: 64 (over y, x_lo, z), rep: 4 (over x_hi, core).
Axes of the slice: x: 4 (x_hi: 2, x_lo: 2; x = x_hi * 2 + x_lo), y: 4, z: 8, core: 2. Of those that a mesh axis runs over, the one named last changes fastest.
Arguments:
- records: bfloat16 [2, 64, 256, 2048], P(None, None, 'rep', 'chan'), may hold values from -6 to 6
- sources: int32 [128], replicated, may hold values from 0 to 16383
- dead_list: int32 [2, 1024], replicated, may hold values from 0 to 16383
Outputs:
- correlations: float32 [128, 64, 16384], P('rep', None, 'chan')
All inputs are finite; a program needn't handle non-finite values.
Results may differ from a plain program's by a relative error of at most 0.0072.
Values may be sent and summed in bfloat16 or wider, within the bound.
A program may use at most 64 MiB of HBM per device.

v0:
```python
import math

import jax
import jax.numpy as jnp
from jax import lax
from jax.sharding import PartitionSpec as P

WINDOW_SAMPLES = 2048
K = 256
K0 = 16
HALF = 32
WH = 32
LAGS = 64


tile_span = 128
tiny_eps = 1e-06


def live_table(dead_list, total):
    window_count, listed = dead_list.shape
    window_rows = jnp.broadcast_to(
        jnp.arange(window_count, dtype=jnp.int32)[:, None], (window_count, listed)
    )
    return jnp.ones((window_count, total), jnp.float32).at[window_rows, dead_list].set(0.0)


def running_mean(records):
    length = records.shape[-1]
    blocks = length // tile_span
    leading = records.shape[:-1]
    magnitude = jnp.abs(records)
    padded = jnp.pad(magnitude, [(0, 0)] * (records.ndim - 1) + [(tile_span, tile_span)])
    before = padded[..., :length].reshape(leading + (blocks, tile_span))
    middle = magnitude.reshape(leading + (blocks, tile_span))
    after = padded[..., 2 * tile_span :].reshape(leading + (blocks, tile_span))
    views = jnp.concatenate([before, middle, after], axis=-1).reshape(-1, 3 * tile_span)
    offsets = jnp.arange(3 * tile_span, dtype=jnp.int32)[:, None] - tile_span
    targets = jnp.arange(tile_span, dtype=jnp.int32)[None, :]
    band_unit_mask = (jnp.abs(offsets - targets) <= HALF).astype(jnp.bfloat16)
    totals = jnp.dot(views, band_unit_mask, preferred_element_type=jnp.float32).reshape(
        leading + (length,)
    )
    sample = jnp.arange(length, dtype=jnp.int32)
    counts = (jnp.minimum(sample, HALF) + jnp.minimum(length - 1 - sample, HALF) + 1).astype(
        jnp.float32
    )
    return totals / counts


def dft_table(length):
    sample = jnp.arange(length, dtype=jnp.int32)[:, None]
    bin_index = K0 + jnp.arange(K, dtype=jnp.int32)[None, :]
    phase = sample * bin_index % length
    angle = phase.astype(jnp.float32) * (2.0 * math.pi / length)
    return jnp.concatenate([jnp.cos(angle), -jnp.sin(angle)], axis=1).astype(jnp.bfloat16)


def whiten(spectrum):
    real_part = spectrum[:, :K]
    imag_part = spectrum[:, K:]
    amplitude = jnp.sqrt(real_part * real_part + imag_part * imag_part)
    index_row = jnp.arange(K, dtype=jnp.int32)[:, None]
    index_col = jnp.arange(K, dtype=jnp.int32)[None, :]
    band = (jnp.abs(index_row - index_col) <= WH).astype(jnp.float32)
    smoothed_amplitude = jnp.dot(amplitude, band, precision=lax.Precision.HIGHEST) / jnp.sum(
        band, axis=0
    )
    return (
        spectrum / (jnp.concatenate([smoothed_amplitude, smoothed_amplitude], axis=1) + tiny_eps)
    ).astype(jnp.bfloat16)


def preprocess(records):
    mean_abs = running_mean(records)
    normed = (records.astype(jnp.float32) / (mean_abs + tiny_eps)).astype(jnp.bfloat16)
    spectrum = jnp.dot(normed, dft_table(records.shape[-1]), preferred_element_type=jnp.float32)
    return whiten(spectrum)


def lag_kernel(source_spectrum):
    bin_index = K0 + jnp.arange(K, dtype=jnp.int32)[None, :]
    lag_index = jnp.arange(LAGS, dtype=jnp.int32)[:, None] - LAGS // 2
    phase = jnp.mod(lag_index * bin_index, WINDOW_SAMPLES)
    angle = phase.astype(jnp.float32) * (2.0 * math.pi / WINDOW_SAMPLES)
    cosine_lookup = jnp.cos(angle)[None, :, None, :]
    sin_table = jnp.sin(angle)[None, :, None, :]
    real_part = source_spectrum[:, None, :, :K].astype(jnp.float32)
    imag_part = source_spectrum[:, None, :, K:].astype(jnp.float32)
    with_real = real_part * cosine_lookup + imag_part * sin_table
    with_imag = imag_part * cosine_lookup - real_part * sin_table
    return jnp.concatenate([with_real, with_imag], axis=3).astype(jnp.bfloat16)


def correlate(kernel, spectra, source_live, chan_live):
    summed = lax.dot_general(
        kernel, spectra, (((2, 3), (0, 2)), ((), ())), preferred_element_type=jnp.float32
    )
    pairs = jnp.dot(source_live.T, chan_live, precision=lax.Precision.HIGHEST)
    return summed / (math.sqrt(K) * jnp.maximum(pairs, 1.0))[:, None, :]


def shards(records, sources, dead_list):
    window_count, groups, ch_width, span_len = records.shape
    reps = lax.axis_size("rep")
    chan_place = lax.axis_index("chan")
    rep_place = lax.axis_index("rep")
    group_share = ch_width * reps
    total = groups * group_share
    live = live_table(dead_list, total)
    group_ids = (
        jnp.arange(groups, dtype=jnp.int32)[:, None] * group_share
        + rep_place * ch_width
        + jnp.arange(ch_width, dtype=jnp.int32)[None, :]
    )
    live_here = live[:, group_ids]
    masked = jnp.where(live_here[..., None] > 0.5, records, jnp.zeros_like(records))
    arrived = lax.all_to_all(masked, "chan", split_axis=1, concat_axis=3, tiled=True)
    flat_rows = arrived.reshape(-1, arrived.shape[-1])
    spectra = preprocess(flat_rows).reshape(arrived.shape[0], ch_width, 2 * K)
    own_ids = (
        chan_place * group_share + rep_place * ch_width + jnp.arange(ch_width, dtype=jnp.int32)
    )
    onehot = (sources[:, None] == own_ids[None, :]).astype(jnp.bfloat16)
    picked = jnp.einsum("sc,wcf->swf", onehot, spectra, preferred_element_type=jnp.float32)
    quarter = sources.shape[0] // reps
    summed = lax.psum(picked, ("chan", "rep"))
    mine = lax.dynamic_slice_in_dim(summed, rep_place * quarter, quarter, 0)
    source_spectrum = mine.astype(jnp.bfloat16)
    source_live = live[:, sources]
    kernel = lag_kernel(source_spectrum)
    quarter_live = lax.dynamic_slice_in_dim(source_live, rep_place * quarter, quarter, 1)
    piece = lax.all_gather(spectra, "rep", axis=1, tiled=True)
    piece_ids = chan_place * group_share + jnp.arange(piece.shape[1], dtype=jnp.int32)
    return correlate(kernel, piece, quarter_live, live[:, piece_ids])


def solution(mesh):
    placed = (P(None, None, "rep", "chan"), P(), P())
    return jax.shard_map(
        shards, mesh=mesh, in_specs=placed, out_specs=P("rep", None, "chan"), check_vma=False
    )
```

profile of v0, /device:TPU:1, one launch (start us, length us, event | category | flops | bytes accessed | tf_op | source)
XLA Modules:
  0.0 189.5 jit_solution(2742913124565968528)
XLA Ops:
  2.4 8.1 %scatter_custom_fusion = f32[32768]{0:T(1024)S(1)} fusion(s32[2048]{0:T(1024)S(1)} %bitcast.50, f32[2048]{0:T(1024)S(1)} %broadcast.257, f32[]{:T(128)} %constant.27.clone.1), kind=kCustom, calls=%fused_computation.68 | custom fusion | bytes 131076
  10.6 5.0 %copy.42 = f32[2,16384]{0,1:T(8,128)} copy(f32[2,16384]{1,0:T(2,128)S(1)} %reshape.212) | data formatting | bytes 262144 | tf_op jit(solution)/shard_map/scatter | solution.py:25
  15.6 14.1 %gather_fusion = f32[4096,2]{1,0:T(8,128)S(1)} fusion(f32[2,16384]{0,1:T(8,128)} %copy.42, s32[4096]{0:T(1024)S(1)} %broadcast_clamp_fusion), kind=kCustom, calls=%fused_computation | custom fusion | bytes 81920 | tf_op jit(solution)/shard_map/gather | solution.py:116
  30.7 1.4 fusion.59
  32.1 1.5 reshape.254
  33.6 13.8 %all-to-all-start = ((bf16[64,2,2048]{2,1,0:T(2,128)(2,1)}), bf16[64,2,2048]{2,1,0:T(2,128)(2,1)S(1)}, u32[]{:S(2)}, u32[]{:S(2)}) async-start(bf16[64,2,2048]{2,1,0:T(2,128)(2,1)} %reshape.254), calls=%async_computation | async-start | bytes 1048576 | tf_op jit(solution)/shard_map/all_to_all | solution.py:118
  47.6 4.0 %gather_fusion.1 = f32[128,2]{1,0:T(8,128)S(1)} fusion(f32[2,16384]{0,1:T(8,128)} %copy.42, s32[1024]{0:T(1024)S(1)} %pad_clamp_fusion.1), kind=kCustom, calls=%fused_computation.1 | custom fusion | bytes 2560 | tf_op jit(solution)/shard_map/gather | solution.py:130
  51.6 4.1 %gather_fusion.2 = f32[256,2]{1,0:T(8,128)S(1)} fusion(f32[2,16384]{0,1:T(8,128)} %copy.42, s32[1024]{0:T(1024)S(1)} %pad_clamp_fusion), kind=kCustom, calls=%fused_computation.2 | custom fusion | bytes 5120 | tf_op jit(solution)/shard_map/gather | solution.py:135
  56.3 9.4 %cosine_convert_fusion = (bf16[2048,256]{1,0:T(8,128)(2,1)}, bf16[2048,256]{1,0:T(8,128)(2,1)}) fusion(s32[256]{0:T(256)S(1)} %iota_add_fusion.1), kind=kLoop, calls=%fused_computation.23 | loop fusion | flops 8912896 | bytes 2098176 | tf_op jit(solution)/shard_map/convert.5
  66.4 1.5 abs_bitcast_fusion
  67.9 2.1 %copy.46 = bf16[2,1,64,64,32]{2,0,4,3,1:T(2,128)(2,1)} copy(bf16[2,1,64,64,32]{2,4,0,3,1:T(8,128)(2,1)S(1)} %get-tuple-element.5) | data formatting | bytes 1048576 | tf_op jit(solution)/shard_map/abs | solution.py:32
  70.0 3.2 %copy.48 = bf16[2,1,64,64,32]{4,3,2,0,1:T(8,128)(2,1)S(1)} copy(bf16[2,1,64,64,32]{2,4,0,3,1:T(8,128)(2,1)S(1)} %get-tuple-element.5) | data formatting | bytes 1048576 | tf_op jit(solution)/shard_map/abs | solution.py:32
  73.2 4.9 %copy.45 = f32[2,1,64,64,32]{2,0,4,3,1:T(2,128)} copy(f32[2,1,64,64,32]{2,4,0,3,1:T(8,128)} %get-tuple-element.6) | data formatting | bytes 2097152 | tf_op jit(solution)/shard_map/convert_element_type | solution.py:76
  78.1 3.4 %reshape.213 = f32[128,2048]{0,1:T(8,128)} reshape(f32[2,1,64,64,32]{2,0,4,3,1:T(2,128)} %copy.45) | data formatting | bytes 2097152 | tf_op jit(solution)/shard_map/convert_element_type | solution.py:76
  81.5 1.3 abs.30
  82.8 1.2 pad_slice_fusion.1
  85.0 2.1 %concatenate.23 = bf16[2048,128]{1,0:T(8,128)(2,1)} reshape(bf16[128,2048]{1,0:T(8,128)(2,1)} %copy.47) | data formatting | bytes 1048576 | tf_op jit(solution)/shard_map/concatenate | solution.py:37
  88.4 1.7 abs.31
  90.1 2.0 %fusion.16 = f32[2048,128]{1,0:T(8,128)S(1)} fusion(bf16[2048,128]{1,0:T(8,128)(2,1)} %concatenate.24, bf16[2048,128]{1,0:T(8,128)(2,1)} %abs.31, bf16[2048,128]{1,0:T(8,128)(2,1)} %concatenate.23, s32[384]{0:T(512)S(1)} %iota_add_fusion), kind=kOutput, calls=%fused_computation.27 | convolution fusion | flops 206192640 | bytes 2622976 | tf_op jit(solution)/shard_map/dot_general | solution.py:41
  93.4 2.5 %fusion.7 = f32[128,512]{1,0:T(8,128)S(1)} fusion(bf16[2048,256]{1,0:T(8,128)(2,1)} %get-tuple-element.16, bf16[2048,256]{1,0:T(8,128)(2,1)} %get-tuple-element.15, f32[128,2048]{0,1:T(8,128)S(1)} %copy-done.1, f32[128,2048]{0,1:T(8,128)S(1)} %copy.50, f32[2048]{0:T(1024)S(1)} %fusion.49), kind=kOutput, calls=%fused_computation.16 | convolution fusion | flops 273678336 | bytes 4464640 | tf_op jit(solution)/shard_map/dot_general | solution.py:77
  96.2 9.4 %all_gather.3 = bf16[2,256,512]{2,1,0:T(8,128)(2,1)S(1)} all-gather(bf16[2,64,512]{2,1,0:T(8,128)(2,1)S(1)} %bitcast.48), channel_id=1, replica_groups=mesh['chan'=64,'rep'=4] {'rep'}, dimensions={1}, use_global_device_ids=true | all-gather | bytes 655360 | tf_op jit(solution)/shard_map/all_gather | solution.py:133
  106.0 79.2 %all-reduce.2 = bf16[128,2,512]{2,0,1:T(8,128)(2,1)S(1)} all-reduce(f32[128,2,512]{2,0,1:T(8,128)S(1)} %fusion.41), channel_id=1, replica_groups=mesh['chan'=64,'rep'=4] {'chan','rep'}, use_global_device_ids=true, to_apply=%region_2.3 | all-reduce | flops 131072 | bytes 786432 | tf_op jit(solution)/shard_map/psum | solution.py:127
  185.4 1.5 add_convert_fusion
  186.9 2.7 %bitcast_divide_fusion = f32[32,64,256]{2,1,0:T(8,128)} fusion(bf16[32,64,2,256]{3,1,2,0:T(8,128)(2,1)S(1)} %get-tuple-element.10, bf16[32,64,2,256]{3,1,2,0:T(8,128)(2,1)S(1)} %get-tuple-element.9, f32[32,256]{1,0:T(8,128)S(1)} %fusion.22, bf16[2,256,512]{2,1,0:T(8,128)(2,1)S(1)} %all_gather.3), kind=kOutput, calls=%fused_computation.21 | convolution fusion | flops 1082654720 | bytes 6848512 | tf_op jit(solution)/shard_map/dot_general | solution.py:96
  (46 shorter events, 9.1 us)
Async XLA Ops:
  30.7 16.8 %copy-start.2 = (s32[128]{0:T(128)S(1)}, s32[128]{0:T(128)}, u32[]{:S(2)}) copy-start(s32[128]{0:T(128)} %param.4) | copy-start | bytes 1540
  33.6 32.1 %all-to-all-start = ((bf16[64,2,2048]{2,1,0:T(2,128)(2,1)}), bf16[64,2,2048]{2,1,0:T(2,128)(2,1)S(1)}, u32[]{:S(2)}, u32[]{:S(2)}) async-start(bf16[64,2,2048]{2,1,0:T(2,128)(2,1)} %reshape.254), calls=%async_computation | async-start | bytes 1048576 | tf_op jit(solution)/shard_map/all_to_all | solution.py:118
  78.1 3.4 %copy-start = (bf16[2,1,64,64,32]{2,0,4,3,1:T(2,128)(2,1)S(1)}, bf16[2,1,64,64,32]{2,0,4,3,1:T(2,128)(2,1)}, u32[]{:S(2)}) copy-start(bf16[2,1,64,64,32]{2,0,4,3,1:T(2,128)(2,1)} %copy.46) | copy-start | bytes 1572868
  92.1 1.2 copy-start.1
where the time goes:
time: 190 us
  blocking collectives  88.6 us (47%)
  local copies, waits for them, and re-layouts  62 us (33%)
  other arithmetic  16.8 us (9%)
  starting transfers between devices  13.8 us (7%)
  matrix products  8.04 us (4%)
    psum x1, blocking collectives, shards(): summed = lax.psum(picked, ('chan', 'rep'))  79.2 us
    gather x1, local copies, waits for them, and re-layouts, shards(): live_here = live[:, group_ids]  14.1 us
    all_to_all x1, starting transfers between devices, shards(): lax.all_to_all(masked, 'chan', split_axis=1, concat_axis=3, tiled=True)  13.8 us
    unnamed x11, local copies, waits for them, and re-layouts  11 us
    another operation x2, other arithmetic  10.9 us
    all_gather x1, blocking collectives, shards(): piece = lax.all_gather(spectra, 'rep', axis=1, tiled=True)  9.42 us
    abs x4, local copies, waits for them, and re-layouts, running_mean(): magnitude = jnp.abs(records)  8.32 us
    convert_element_type x2, local copies, waits for them, and re-layouts, preprocess(): records.astype(jnp.float32) / (mean_abs + tiny_eps)  8.27 us
  transfers between devices with their start and end apart: 1, of which 0 were waited for; matrix products, arithmetic and copies ran while one was open for 10% of the time, Pallas kernels for 0%

commit v1 on v0

v1 whole, which is shorter than its diff:
```python
import functools
import math

import jax
import jax.numpy as jnp
import numpy as np
from jax import lax
from jax.experimental import pallas as pl
from jax.experimental.pallas import tpu as pltpu
from jax.sharding import PartitionSpec as P

WINDOW_SAMPLES = 2048
K = 256
K0 = 16
HALF = 32
WH = 32
LAGS = 64
EPS = 1e-06
Z = 8

MESH = pl.DeviceIdType.MESH
BF16 = jnp.bfloat16
F32 = jnp.float32


def tables(length):
    m = ((K0 + np.arange(K))[:, None] * np.arange(length)[None, :]) % length
    angle = m.astype(np.float64) * (2.0 * math.pi / length)
    dft = np.concatenate([np.cos(angle), -np.sin(angle)], axis=0).astype(jnp.bfloat16)
    row, col = np.arange(128)[:, None], np.arange(256)[None, :]
    band = (np.abs(col - 64 - row) <= HALF).astype(jnp.bfloat16)
    j = np.arange(K)
    smooth = (np.abs(j[:, None] - j[None, :]) <= WH).astype(np.float32)
    count = np.broadcast_to(1.0 / smooth.sum(axis=1, keepdims=True), (K, 128)).astype(np.float32)
    tau = np.arange(LAGS)[:, None] - LAGS // 2
    phi = ((tau * (K0 + j)[None, :]) % length).astype(np.float64) * (2.0 * math.pi / length)
    lag = np.stack([np.cos(phi), np.sin(phi)]).astype(np.float32)
    return dft, band, smooth.astype(jnp.bfloat16), count, lag


def lane_iota(shape):
    return lax.broadcasted_iota(jnp.int32, shape, len(shape) - 1)


def whiten(load_rows, dft, band, smooth, count, absbuf, normed):
    length = normed.shape[0]
    blocks = length // 128
    zero = jnp.zeros((64, 128), BF16)
    absbuf[0:64, :] = zero
    absbuf[64 + length :, :] = zero

    def fill(b, carry):
        absbuf[pl.ds(pl.multiple_of(64 + b * 128, 64), 128), :] = jnp.abs(load_rows(b))
        return carry

    lax.fori_loop(0, blocks, fill, 0)

    def norm(b, carry):
        start = pl.multiple_of(b * 128, 128)
        total = jnp.dot(band[...], absbuf[pl.ds(start, 256), :], preferred_element_type=F32)
        t = lax.broadcasted_iota(jnp.int32, (128, 128), 0) + b * 128
        n = (jnp.minimum(t, HALF) + jnp.minimum(length - 1 - t, HALF) + 1).astype(F32)
        x = load_rows(b).astype(F32)
        normed[pl.ds(start, 128), :] = (x * n / (total + EPS * n)).astype(BF16)
        return carry

    lax.fori_loop(0, blocks, norm, 0)
    spectrum = jnp.dot(dft[...], normed[...], preferred_element_type=F32)
    re, im = spectrum[:K], spectrum[K:]
    amp = jnp.sqrt(re * re + im * im)
    high = amp.astype(BF16)
    rest = amp - high.astype(F32)
    mid = rest.astype(BF16)
    low = (rest - mid.astype(F32)).astype(BF16)
    s = smooth[...]
    total = (
        jnp.dot(s, low, preferred_element_type=F32)
        + jnp.dot(s, mid, preferred_element_type=F32)
        + jnp.dot(s, high, preferred_element_type=F32)
    )
    scale = 1.0 / (total * count[...] + EPS)
    return re * scale, im * scale


def gather_kernel(
    chans, reps,
    rec_hbm, src_ref, dead_ref, dft_hbm, band, smooth, count, lag,
    rhs_out, lk_out, inv_out,
    rec, dft, packed, recv, picks, pickrecv, srcbuf, own, gath, absbuf, normed, srcspec, livesrc,
    sem_in, sem_dft, a_send, a_recv, p_send, p_recv, z_send, z_recv, y_send, y_recv, g_send, g_recv,
):
    c, r = lax.axis_index("chan"), lax.axis_index("rep")
    z, yx = lax.rem(c, Z), c // Z
    nyx = chans // Z
    barrier = pltpu.get_barrier_semaphore()

    load = pltpu.make_async_copy(rec_hbm, rec, sem_in)
    load.start()
    load_dft = pltpu.make_async_copy(dft_hbm, dft, sem_dft)
    load_dft.start()

    def greet(k, carry):
        pl.semaphore_signal(barrier, inc=1, device_id={"chan": lax.rem(c + k, chans), "rep": r}, device_id_type=MESH)
        return carry

    lax.fori_loop(1, chans, greet, 0)
    for k in range(1, reps):
        pl.semaphore_signal(barrier, inc=1, device_id={"chan": c, "rep": lax.rem(r + k, reps)}, device_id_type=MESH)

    load.wait()

    def pack(g, carry):
        packed[g] = jnp.concatenate([rec[0, g], rec[1, g]], axis=1)
        return carry

    lax.fori_loop(0, chans, pack, 0)
    recv[c] = packed[c]
    pl.semaphore_wait(barrier, chans - 1 + reps - 1)

    def send(k, carry):
        d = lax.rem(c + k, chans)
        pltpu.make_async_remote_copy(
            packed.at[d], recv.at[c], a_send, a_recv, device_id={"chan": d, "rep": r}, device_id_type=MESH
        ).start()
        return carry

    lax.fori_loop(1, chans, send, 0)

    src = src_ref[...]
    within = src & 255
    mine = jnp.where((within >> 6) == r, within & 63, -1)
    row = lax.broadcasted_iota(jnp.int32, (128, 128), 0)
    sel = jnp.concatenate(
        [(row == mine).astype(BF16), (row - 64 == jnp.where(mine < 0, -1000, mine)).astype(BF16)], axis=1
    )
    block = src >> 8
    block2 = jnp.concatenate([block, block], axis=1)

    def pick(g, acc):
        part = jnp.dot(packed[g], sel, preferred_element_type=F32)
        return acc + jnp.where(block2 == g, part, 0.0)

    acc = lax.fori_loop(0, chans, pick, jnp.zeros((32, 256), F32))
    lane = lane_iota((32, 128))
    for q in range(reps):
        first = pltpu.roll(acc[:, :128], (128 - 32 * q) % 128, 1)
        second = pltpu.roll(acc[:, 128:], (32 - 32 * q) % 128, 1)
        picks[q] = jnp.where(lane < 32, first, second).astype(BF16)
    pickrecv[r] = picks[r]
    for k in range(1, reps):
        d = lax.rem(r + k, reps)
        pltpu.make_async_remote_copy(
            picks.at[d], pickrecv.at[r], p_send.at[k], p_recv.at[k], device_id={"chan": c, "rep": d}, device_id_type=MESH
        ).start()

    dead = dead_ref[...]
    eye = lax.broadcasted_iota(jnp.int32, (128, 128), 0) == lane_iota((128, 128))
    src_col = jnp.sum(jnp.where(eye, jnp.broadcast_to(src, (128, 128)), 0), axis=1, keepdims=True)
    ones = jnp.ones((8, 1024), BF16)
    chan_live = []
    for w in range(2):
        listed = dead[w : w + 1, :]
        hit = jnp.sum((listed == src_col).astype(F32), axis=1, keepdims=True)
        livesrc[w] = jnp.broadcast_to(jnp.where(hit > 0.5, 0.0, 1.0), (128, 128))
        here = jnp.where((listed >> 8) == c, listed & 255, -1)
        rows = lax.broadcasted_iota(jnp.int32, (256, 1024), 0)
        onehot = (rows == here).astype(BF16)
        hits = lax.dot_general(ones, onehot, (((1,), (1,)), ((), ())), preferred_element_type=F32)
        chan_live.append(jnp.where(hits[0:1] > 0.5, 0.0, 1.0))
    start = pl.multiple_of(r * 32, 32)
    ls = [livesrc[w, pl.ds(start, 32), :] for w in range(2)]
    pairs = jnp.concatenate(
        [
            ls[0] * chan_live[0][:, h * 128 : h * 128 + 128] + ls[1] * chan_live[1][:, h * 128 : h * 128 + 128]
            for h in range(2)
        ],
        axis=1,
    )
    inv_out[...] = 1.0 / (math.sqrt(K) * jnp.maximum(pairs, 1.0))

    for k in range(1, reps):
        d = lax.rem(r + k, reps)
        cp = pltpu.make_async_remote_copy(
            picks.at[d], pickrecv.at[r], p_send.at[k], p_recv.at[k], device_id={"chan": c, "rep": d}, device_id_type=MESH
        )
        cp.wait_send()
        cp.wait_recv()
    total = pickrecv[0].astype(F32)
    for q in range(1, reps):
        total = total + pickrecv[q].astype(F32)
    half = jnp.where(lane[:16] < 64, total[:16], pltpu.roll(total[16:], 64, 1))
    srcbuf[c] = half.astype(BF16)

    def z_copy(k):
        return pltpu.make_async_remote_copy(
            srcbuf.at[c], srcbuf.at[c], z_send, z_recv,
            device_id={"chan": yx * Z + lax.rem(z + k, Z), "rep": r}, device_id_type=MESH,
        )

    def z_start(k, carry):
        z_copy(k).start()
        return carry

    lax.fori_loop(1, Z, z_start, 0)
    some = srcbuf.at[pl.ds(0, Z - 1)]
    bulk = pltpu.make_async_remote_copy(
        some, some, z_send, z_recv, device_id={"chan": c, "rep": lax.rem(r + 1, reps)}, device_id_type=MESH
    )
    bulk.wait_send()
    bulk.wait_recv()

    def y_start(k, carry):
        span = srcbuf.at[pl.ds(yx * Z, Z)]
        pltpu.make_async_remote_copy(
            span, span, y_send, y_recv,
            device_id={"chan": lax.rem(yx + k, nyx) * Z + z, "rep": r}, device_id_type=MESH,
        ).start()
        return carry

    lax.fori_loop(1, nyx, y_start, 0)
    some = srcbuf.at[pl.ds(0, (nyx - 1) * Z)]
    bulk = pltpu.make_async_remote_copy(
        some, some, y_send, y_recv, device_id={"chan": c, "rep": lax.rem(r + 1, reps)}, device_id_type=MESH
    )
    bulk.wait_send()
    bulk.wait_recv()

    load_dft.wait()

    def source_rows(b):
        parts = []
        for i in range(4):
            piece = srcbuf[b * 4 + i]
            parts += [piece, pltpu.roll(piece.astype(F32), 64, 1).astype(BF16)]
        return jnp.concatenate(parts, axis=0)

    re, im = whiten(source_rows, dft, band, smooth, count, absbuf, normed)
    ls_col = jnp.concatenate([ls[0], ls[1]], axis=0)[:, :1]
    for part, value in enumerate((re, im)):
        rows = jnp.transpose(value)[:64] * ls_col
        srcspec[part] = rows.astype(BF16).astype(F32)

    def lag_rows(s, carry):
        at = pl.multiple_of(s * LAGS, LAGS)
        for w in range(2):
            u = srcspec[0, pl.ds(w * 32 + s, 1), :]
            v = srcspec[1, pl.ds(w * 32 + s, 1), :]
            cos, sin = lag[0], lag[1]
            lk_out[pl.ds(at, LAGS), w * 512 : w * 512 + 256] = (u * cos + v * sin).astype(BF16)
            lk_out[pl.ds(at, LAGS), w * 512 + 256 : w * 512 + 512] = (v * cos - u * sin).astype(BF16)
        return carry

    lax.fori_loop(0, 32, lag_rows, 0)

    some = recv.at[pl.ds(0, chans - 1)]
    bulk = pltpu.make_async_remote_copy(
        packed.at[pl.ds(0, chans - 1)], some, a_send, a_recv,
        device_id={"chan": c, "rep": lax.rem(r + 1, reps)}, device_id_type=MESH,
    )
    bulk.wait_send()
    bulk.wait_recv()

    def own_rows(b):
        return jnp.concatenate([recv[b * 4 + i] for i in range(4)], axis=0)

    re, im = whiten(own_rows, dft, band, smooth, count, absbuf, normed)
    halves = []
    for w in range(2):
        quarter = jnp.zeros((1, 128), F32)
        for q in range(reps):
            tile = chan_live[w][:, (q // 2) * 128 : (q // 2) * 128 + 128]
            quarter = jnp.where(r == q, pltpu.roll(tile, (64 * (w - q)) % 128, 1), quarter)
        halves.append(quarter)
    mask = jnp.where(lane_iota((1, 128)) < 64, halves[0], halves[1])
    own[0:K, :] = (re * mask).astype(BF16)
    own[K:, :] = (im * mask).astype(BF16)
    gath[r] = own[...]

    def g_copy(k):
        return pltpu.make_async_remote_copy(
            own, gath.at[r], g_send.at[k], g_recv.at[k],
            device_id={"chan": c, "rep": lax.rem(r + k, reps)}, device_id_type=MESH,
        )

    for k in range(1, reps):
        g_copy(k).start()
    for k in range(1, reps):
        cp = g_copy(k)
        cp.wait_send()
        cp.wait_recv()
    low = lane_iota((512, 128)) < 64
    for h in range(2):
        a, b = gath[2 * h].astype(F32), gath[2 * h + 1].astype(F32)
        rhs_out[0:512, h * 128 : h * 128 + 128] = jnp.where(low, a, pltpu.roll(b, 64, 1)).astype(BF16)
        rhs_out[512:1024, h * 128 : h * 128 + 128] = jnp.where(low, pltpu.roll(a, 64, 1), b).astype(BF16)


def correlate_kernel(lk, rhs, inv, out):
    step = pl.program_id(0)
    summed = jnp.dot(lk[...], rhs[...], preferred_element_type=F32)
    for i in range(out.shape[0]):
        out[i] = summed[i * LAGS : (i + 1) * LAGS] * inv[pl.ds(step * out.shape[0] + i, 1), :]


def solution(mesh):
    chans, reps = mesh.shape["chan"], mesh.shape["rep"]

    def shards(records, sources, dead_list):
        windows, groups, width, span = records.shape
        length = span * chans
        dft, band, smooth, count, lag = tables(length)
        quarter = sources.shape[0] // reps
        vmem = pl.BlockSpec(memory_space=pltpu.VMEM)
        anyspace = pl.BlockSpec(memory_space=pl.ANY)
        dma = pltpu.SemaphoreType.DMA
        rhs, lk, inv = pl.pallas_call(
            functools.partial(gather_kernel, chans, reps),
            out_shape=[
                jax.ShapeDtypeStruct((1024, 256), BF16),
                jax.ShapeDtypeStruct((quarter * LAGS, 1024), BF16),
                jax.ShapeDtypeStruct((quarter, 256), F32),
            ],
            in_specs=[anyspace, vmem, vmem, anyspace, vmem, vmem, vmem, vmem],
            out_specs=[vmem] * 3,
            scratch_shapes=[
                pltpu.VMEM((windows, groups, span, width), BF16),
                pltpu.VMEM((512, length), BF16),
                pltpu.VMEM((chans, span, 128), BF16),
                pltpu.VMEM((chans, span, 128), BF16),
                pltpu.VMEM((reps, span, 128), BF16),
                pltpu.VMEM((reps, span, 128), BF16),
                pltpu.VMEM((chans, 16, 128), BF16),
                pltpu.VMEM((512, 128), BF16),
                pltpu.VMEM((reps, 512, 128), BF16),
                pltpu.VMEM((length + 128, 128), BF16),
                pltpu.VMEM((length, 128), BF16),
                pltpu.VMEM((2, 64, 256), F32),
                pltpu.VMEM((2, 128, 128), F32),
                dma, dma, dma, dma, dma((reps,)), dma((reps,)), dma, dma, dma, dma, dma((reps,)), dma((reps,)),
            ],
            compiler_params=pltpu.CompilerParams(
                collective_id=0, has_side_effects=True, vmem_limit_bytes=48 << 20
            ),
            name="gather_spectra",
        )(
            jnp.transpose(records, (0, 1, 3, 2)),
            sources.reshape(1, -1),
            dead_list,
            jnp.asarray(dft),
            jnp.asarray(band),
            jnp.asarray(smooth),
            jnp.asarray(count),
            jnp.asarray(lag),
        )
        step = 4
        return pl.pallas_call(
            correlate_kernel,
            grid=(quarter // step,),
            out_shape=jax.ShapeDtypeStruct((quarter, LAGS, 256), F32),
            in_specs=[
                pl.BlockSpec((step * LAGS, 1024), lambda i: (i, 0)),
                pl.BlockSpec((1024, 256), lambda i: (0, 0)),
                pl.BlockSpec((quarter, 256), lambda i: (0, 0)),
            ],
            out_specs=pl.BlockSpec((step, LAGS, 256), lambda i: (i, 0, 0)),
            name="correlate",
        )(lk, rhs, inv)

    return jax.shard_map(
        shards,
        mesh=mesh,
        in_specs=(P(None, None, "rep", "chan"), P(), P()),
        out_specs=P("rep", None, "chan"),
        check_vma=False,
    )
```

time: 190 us -> 72.3 us (0.38)
  blocking collectives: 88.6 us -> 0 us
  Pallas kernels: 0 us -> 62.7 us
  local copies, waits for them, and re-layouts: 62 us -> 9.12 us
  other arithmetic: 16.8 us -> 0 us
  starting transfers between devices: 13.8 us -> 0 us
  matrix products: 8.04 us -> 0 us
    psum x1 -> x0, blocking collectives: 79.2 us -> none  [shards(): summed = lax.psum(picked, ('chan', 'rep'))]
    pallas_call x0 -> x2, Pallas kernels: none -> 62.7 us  [the longest x1 55.4 us: shards(): pl.pallas_call(functools.partial(gather_kernel, chans, reps), out_shape=[...]
    gather x3 -> x0, local copies, waits for them, and re-layouts: 22.3 us -> none  [the longest x1 14.1 us: shards(): live_here = live[:, group_ids]]
    all_to_all x1 -> x0, starting transfers between devices: 13.8 us -> none  [shards(): lax.all_to_all(masked, 'chan', split_axis=1, concat_axis=3, tiled=True)]
    another operation x2 -> x0, other arithmetic: 10.9 us -> none
    all_gather x1 -> x0, blocking collectives: 9.42 us -> none  [shards(): piece = lax.all_gather(spectra, 'rep', axis=1, tiled=True)]
    convert_element_type x5 -> x0, local copies, waits for them, and re-layouts: 8.39 us -> none  [the longest x2 8.27 us: preprocess(): records.astype(jnp.float32) / (mean_abs + tiny_eps)]
    abs x4 -> x0, local copies, waits for them, and re-layouts: 8.32 us -> none  [running_mean(): magnitude = jnp.abs(records)]
  transfers between devices with their start and end apart: 1 -> 0, of which waited for: 0 -> 0; matrix products, arithmetic and copies ran while one was open for 10% -> 0% of each run, Pallas kernels for 0% -> 0%
where the time goes in v1:
time: 72.3 us; the launch traced here: 71.9 us
  Pallas kernels  62.7 us (87%)
  local copies, waits for them, and re-layouts  9.12 us (13%)
    pallas_call x1, Pallas kernels, shards(): pl.pallas_call(functools.partial(gather_kernel, chans, reps), out_shape=[...  55.4 us
    unnamed x20, local copies, waits for them, and re-layouts  9.12 us
    pallas_call x1, Pallas kernels, shards(): pl.pallas_call(correlate_kernel, grid=(quarter // step,), out_shape=jax.S...  7.28 us

profile of v1, /device:TPU:1, one launch (start us, length us, event | category | flops | bytes accessed | tf_op | source)
XLA Modules:
  0.0 71.9 jit_solution(17985303036699928262)
XLA Ops:
  0.0 0.0 copy-start
  0.0 1.6 %copy-done = bf16[512,2048]{1,0:T(8,128)(2,1)S(1)} copy-done((bf16[512,2048]{1,0:T(8,128)(2,1)S(1)}, bf16[512,2048]{1,0:T(8,128)(2,1)}, u32[]{:S(2)}) %copy-start) | copy-done | bytes 2097176
  1.6 0.0 copy-start.1
  1.6 1.2 %copy-done.1 = bf16[2,64,64,32]{2,3,1,0:T(8,128)(2,1)S(1)} copy-done((bf16[2,64,64,32]{2,3,1,0:T(8,128)(2,1)S(1)}, bf16[2,64,64,32]{2,3,1,0:T(8,128)(2,1)}, u32[]{:S(2)}) %copy-start.1) | copy-done | bytes 524312
  2.8 0.0 copy-start.3
  2.8 0.9 %copy-done.3 = f32[2,64,256]{2,1,0:T(8,128)S(1)} copy-done((f32[2,64,256]{2,1,0:T(8,128)S(1)}, f32[2,64,256]{2,1,0:T(8,128)}, u32[]{:S(2)}) %copy-start.3) | copy-done | bytes 131096
  3.7 0.0 copy-start.4
  3.7 0.9 %copy-done.4 = f32[256,128]{1,0:T(8,128)S(1)} copy-done((f32[256,128]{1,0:T(8,128)S(1)}, f32[256,128]{1,0:T(8,128)}, u32[]{:S(2)}) %copy-start.4) | copy-done | bytes 131096
  4.6 0.0 copy-start.5
  4.6 0.9 %copy-done.5 = bf16[256,256]{1,0:T(8,128)(2,1)S(1)} copy-done((bf16[256,256]{1,0:T(8,128)(2,1)S(1)}, bf16[256,256]{1,0:T(8,128)(2,1)}, u32[]{:S(2)}) %copy-start.5) | copy-done | bytes 131096
  5.5 0.0 copy-start.6
  5.5 0.8 %copy-done.6 = bf16[128,256]{1,0:T(8,128)(2,1)S(1)} copy-done((bf16[128,256]{1,0:T(8,128)(2,1)S(1)}, bf16[128,256]{1,0:T(8,128)(2,1)}, u32[]{:S(2)}) %copy-start.6) | copy-done | bytes 65560
  6.4 0.0 copy-start.8
  6.4 0.7 copy-done.8
  7.1 0.0 copy-start.9
  7.1 0.7 copy-done.9
  7.7 55.4 %gather_spectra.1 = (bf16[1024,256]{1,0:T(8,128)(2,1)S(1)}, bf16[2048,1024]{1,0:T(8,128)(2,1)}, f32[32,256]{1,0:T(8,128)S(1)}) custom-call(bf16[2,64,32,64]{3,2,1,0:T(8,128)(2,1)S(1)} %bitcast.2, s32[1,128]{1,0:T(1,128)S(1)} %bitcast.3, s32[2,1024]{1,0:T(2,128)S(1)} %copy-done.8, bf16[512,2048]{1,0:T(8,128)(2,1)S(1)} %copy-done, ...), custom_call_target="tpu_custom_call" | custom-call | tf_op jit(solution)/shard_map/gather_spectra/pallas_call | solution.py:316
  63.2 0.0 copy-start.2
  63.2 0.8 %copy-done.2 = bf16[1024,256]{1,0:T(8,128)(2,1)} copy-done((bf16[1024,256]{1,0:T(8,128)(2,1)}, bf16[1024,256]{1,0:T(8,128)(2,1)S(1)}, u32[]{:S(2)}) %copy-start.2) | copy-done | bytes 524312
  64.0 0.0 copy-start.7
  64.0 0.6 copy-done.7
  64.6 7.3 %correlate.1 = f32[32,64,256]{2,1,0:T(8,128)} custom-call(bf16[2048,1024]{1,0:T(8,128)(2,1)} %get-tuple-element.8.lk, bf16[1024,256]{1,0:T(8,128)(2,1)} %copy-done.2, f32[32,256]{1,0:T(8,128)} %copy-done.7), custom_call_target="tpu_custom_call" | custom-call | tf_op jit(solution)/shard_map/correlate/pallas_call | solution.py:356
Async XLA Ops:
  0.0 1.6 %copy-start = (bf16[512,2048]{1,0:T(8,128)(2,1)S(1)}, bf16[512,2048]{1,0:T(8,128)(2,1)}, u32[]{:S(2)}) copy-start(bf16[512,2048]{1,0:T(8,128)(2,1)} %constant.10.clone.dft_hbm) | copy-start | bytes 6291460
  1.6 1.2 %copy-start.1 = (bf16[2,64,64,32]{2,3,1,0:T(8,128)(2,1)S(1)}, bf16[2,64,64,32]{2,3,1,0:T(8,128)(2,1)}, u32[]{:S(2)}) copy-start(bf16[2,64,64,32]{2,3,1,0:T(8,128)(2,1)} %param.8) | copy-start | bytes 1572868
  2.8 0.9 %copy-start.3 = (f32[2,64,256]{2,1,0:T(8,128)S(1)}, f32[2,64,256]{2,1,0:T(8,128)}, u32[]{:S(2)}) copy-start(f32[2,64,256]{2,1,0:T(8,128)} %constant.14.clone.lag) | copy-start | bytes 393220
  3.7 0.9 %copy-start.4 = (f32[256,128]{1,0:T(8,128)S(1)}, f32[256,128]{1,0:T(8,128)}, u32[]{:S(2)}) copy-start(f32[256,128]{1,0:T(8,128)} %constant.13.clone.count) | copy-start | bytes 393220
  4.6 0.9 %copy-start.5 = (bf16[256,256]{1,0:T(8,128)(2,1)S(1)}, bf16[256,256]{1,0:T(8,128)(2,1)}, u32[]{:S(2)}) copy-start(bf16[256,256]{1,0:T(8,128)(2,1)} %constant.12.clone.smooth) | copy-start | bytes 393220
  5.5 0.8 %copy-start.6 = (bf16[128,256]{1,0:T(8,128)(2,1)S(1)}, bf16[128,256]{1,0:T(8,128)(2,1)}, u32[]{:S(2)}) copy-start(bf16[128,256]{1,0:T(8,128)(2,1)} %constant.11.clone.band) | copy-start | bytes 196612
  6.4 0.7 copy-start.8
  7.1 0.7 copy-start.9
  63.2 0.8 %copy-start.2 = (bf16[1024,256]{1,0:T(8,128)(2,1)}, bf16[1024,256]{1,0:T(8,128)(2,1)S(1)}, u32[]{:S(2)}) copy-start(bf16[1024,256]{1,0:T(8,128)(2,1)S(1)} %get-tuple-element.9.rhs) | copy-start | bytes 1572868
  64.0 0.6 copy-start.7

commit v2 on v1

v2 whole, which is shorter than its diff:
```python
import functools
import math

import jax
import jax.numpy as jnp
import numpy as np
from jax import lax
from jax.experimental import pallas as pl
from jax.experimental.pallas import tpu as pltpu
from jax.sharding import PartitionSpec as P

K = 256
K0 = 16
HALF = 32
WH = 32
LAGS = 64
EPS = 1e-06
Z = 8

MESH = pl.DeviceIdType.MESH
BF16 = jnp.bfloat16
F32 = jnp.float32


def tables(length):
    m = ((K0 + np.arange(K))[:, None] * np.arange(length)[None, :]) % length
    angle = m.astype(np.float64) * (2.0 * math.pi / length)
    dft = np.concatenate([np.cos(angle), -np.sin(angle)], axis=0).astype(jnp.bfloat16)
    tau = np.arange(LAGS)[:, None] - LAGS // 2
    phi = ((tau * (K0 + np.arange(K))[None, :]) % length).astype(np.float64) * (2.0 * math.pi / length)
    lag = np.stack([np.cos(phi), np.sin(phi)]).astype(np.float32)
    return dft, lag


def iota(shape, axis):
    return lax.broadcasted_iota(jnp.int32, shape, axis)


def swap(x):
    return pltpu.roll(x, 64, 1)


def whiten(buf, dft, absbuf, xbuf, normed):
    blocks = buf.shape[0]
    top = blocks * 16
    low = iota((16, 128), 1) < 64

    def spread(b, carry):
        for i in range(8):
            at = b * 8 + i
            first, second = buf[at], buf[at + blocks // 2]
            x0 = jnp.where(low, first, swap(second))
            x1 = jnp.where(low, swap(first), second)
            rows = pl.multiple_of(at * 32, 32)
            xbuf[pl.ds(rows, 16), :] = x0
            xbuf[pl.ds(rows + 16, 16), :] = x1
            absbuf[pl.ds(rows + 64, 16), :] = jnp.abs(x0)
            absbuf[pl.ds(rows + 80, 16), :] = jnp.abs(x1)
        return carry

    lax.fori_loop(0, blocks // 16, spread, 0)
    low = iota((64, 128), 1) < 64
    zero = jnp.zeros((64, 128), BF16)
    absbuf[0:64, :] = jnp.where(low, zero, swap(absbuf[top : top + 64, :]))
    absbuf[top + 64 :, :] = jnp.where(low, swap(absbuf[64:128, :]), zero)
    band = (jnp.abs(iota((128, 256), 1) - 64 - iota((128, 256), 0)) <= HALF).astype(BF16)

    for b in range(top // 128):
        start = b * 128
        total = jnp.dot(band, absbuf[pl.ds(start, 256), :], preferred_element_type=F32)
        t = iota((128, 128), 0) + b * 128 + jnp.where(iota((128, 128), 1) < 64, 0, top)
        n = (jnp.minimum(t, HALF) + jnp.minimum(2 * top - 1 - t, HALF) + 1).astype(F32)
        x = xbuf[pl.ds(start, 128), :].astype(F32)
        normed[pl.ds(start, 128), :] = (x * n / (total + EPS * n)).astype(BF16)
    x = normed[...]
    spectrum = jnp.dot(dft[:, :top], x, preferred_element_type=F32)
    other = jnp.dot(dft[:, top:], x, preferred_element_type=F32)
    spectrum = spectrum + pltpu.roll(other, 64, 1)
    re, im = spectrum[:K], spectrum[K:]
    amp = jnp.sqrt(re * re + im * im)
    high = amp.astype(BF16)
    rest = amp - high.astype(F32)
    mid = rest.astype(BF16)
    near = (jnp.abs(iota((K, K), 0) - iota((K, K), 1)) <= WH).astype(BF16)
    total = jnp.dot(near, mid, preferred_element_type=F32) + jnp.dot(near, high, preferred_element_type=F32)
    j = iota((K, 128), 0)
    n = (jnp.minimum(j, WH) + jnp.minimum(K - 1 - j, WH) + 1).astype(F32)
    scale = 1.0 / (total / n + EPS)
    return re * scale, im * scale


def gather_kernel(
    chans, reps,
    rec_hbm, src_hbm, dead_hbm, dft_hbm, lag_hbm,
    out,
    rec, src_ref, dead_ref, dft, lag,
    packed, recv, cols, picks, pickrecv, srcbuf, gath, rhs, lk, inv, absbuf, xbuf, normed, srcspec, livesrc,
    sem_in, a_send, a_recv, p_send, p_recv, z_send, z_recv, y_send, y_recv, g_send, g_recv,
):
    c, r = lax.axis_index("chan"), lax.axis_index("rep")
    z, yx = lax.rem(c, Z), c // Z
    nyx = chans // Z
    barrier = pltpu.get_barrier_semaphore()

    loads = [
        pltpu.make_async_copy(a, b, sem_in.at[i])
        for i, (a, b) in enumerate(
            [(rec_hbm, rec), (src_hbm, src_ref), (dead_hbm, dead_ref), (dft_hbm, dft), (lag_hbm, lag)]
        )
    ]
    for load in loads:
        load.start()

    def greet(k, carry):
        pl.semaphore_signal(barrier, inc=1, device_id={"chan": lax.rem(c + k, chans), "rep": r}, device_id_type=MESH)
        return carry

    lax.fori_loop(1, chans, greet, 0)
    for k in range(1, reps):
        pl.semaphore_signal(barrier, inc=1, device_id={"chan": c, "rep": lax.rem(r + k, reps)}, device_id_type=MESH)

    loads[0].wait()

    def pack(i, carry):
        for k in range(8):
            g = i * 8 + k
            for w in range(2):
                packed[w, g] = jnp.concatenate([rec[w, g, 0:16], rec[w, g, 16:32]], axis=1)
        return carry

    lax.fori_loop(0, chans // 8, pack, 0)
    for w in range(2):
        recv[w, c] = packed[w, c]

    pl.semaphore_wait(barrier, chans - 1 + reps - 1)

    def send_part(w, first, last):
        def send(k, carry):
            d = lax.rem(c + k, chans)
            pltpu.make_async_remote_copy(
                packed.at[w, d], recv.at[w, c], a_send.at[w], a_recv.at[w],
                device_id={"chan": d, "rep": r}, device_id_type=MESH,
            ).start()
            return carry

        lax.fori_loop(first, last, send, 0)

    send_part(0, 1, chans)

    loads[1].wait()
    src = src_ref[...]
    within = src & 255
    mine = jnp.where((within >> 6) == r, within & 63, -1000)
    row = iota((128, 128), 0)
    sel = jnp.concatenate([(row == mine).astype(BF16), (row - 64 == mine).astype(BF16)], axis=1)
    block = src >> 8
    block2 = jnp.concatenate([block, block], axis=1)
    accs = []
    for w in range(2):
        cols[...] = jnp.dot(packed[w].reshape(chans * 16, 128), sel, preferred_element_type=F32)

        def pick(i, acc):
            for k in range(8):
                g = i * 8 + k
                part = cols[pl.ds(pl.multiple_of(g * 16, 16), 16), :]
                acc = acc + jnp.where(block2 == g, part, 0.0)
            return acc

        accs.append(lax.fori_loop(0, chans // 8, pick, jnp.zeros((16, 256), F32)))
    lane = iota((16, 128), 1)
    for q in range(reps):
        value = jnp.zeros((16, 128), F32)
        for th in range(2):
            for w in range(2):
                to = th * 64 + w * 32
                piece = pltpu.roll(accs[w][:, th * 128 : th * 128 + 128], (to - 32 * q) % 128, 1)
                value = jnp.where((lane >= to) & (lane < to + 32), piece, value)
        picks[q] = value.astype(BF16)
    pickrecv[r] = picks[r]

    def p_copy(k):
        d = lax.rem(r + k, reps)
        return pltpu.make_async_remote_copy(
            picks.at[d], pickrecv.at[r], p_send.at[k], p_recv.at[k], device_id={"chan": c, "rep": d}, device_id_type=MESH
        )

    for k in range(1, reps):
        p_copy(k).start()

    loads[2].wait()
    dead = dead_ref[...]
    eye = iota((128, 128), 0) == iota((128, 128), 1)
    src_col = jnp.sum(jnp.where(eye, jnp.broadcast_to(src, (128, 128)), 0), axis=1, keepdims=True)
    ones = jnp.ones((8, 1024), BF16)
    chan_live = []
    for w in range(2):
        listed = dead[w : w + 1, :]
        hit = jnp.sum((listed == src_col).astype(F32), axis=1, keepdims=True)
        livesrc[w] = jnp.broadcast_to(jnp.where(hit > 0.5, 0.0, 1.0), (128, 128))
        here = jnp.where((listed >> 8) == c, listed & 255, -1)
        onehot = (iota((256, 1024), 0) == here).astype(BF16)
        hits = lax.dot_general(ones, onehot, (((1,), (1,)), ((), ())), preferred_element_type=F32)
        chan_live.append(jnp.where(hits[0:1] > 0.5, 0.0, 1.0))
    start = pl.multiple_of(r * 32, 32)
    ls = [livesrc[w, pl.ds(start, 32), :] for w in range(2)]
    for h in range(2):
        span = slice(h * 128, h * 128 + 128)
        pairs = ls[0] * chan_live[0][:, span] + ls[1] * chan_live[1][:, span]
        inv[:, span] = 1.0 / (math.sqrt(K) * jnp.maximum(pairs, 1.0))

    for k in range(1, reps):
        p_copy(k).wait_send()
        p_copy(k).wait_recv()
    total = pickrecv[0].astype(F32)
    for q in range(1, reps):
        total = total + pickrecv[q].astype(F32)
    srcbuf[c] = total.astype(BF16)

    def z_start(k, carry):
        pltpu.make_async_remote_copy(
            srcbuf.at[c], srcbuf.at[c], z_send, z_recv,
            device_id={"chan": yx * Z + lax.rem(z + k, Z), "rep": r}, device_id_type=MESH,
        ).start()
        return carry

    def y_start(k, carry):
        span = srcbuf.at[pl.ds(yx * Z, Z)]
        pltpu.make_async_remote_copy(
            span, span, y_send, y_recv,
            device_id={"chan": lax.rem(yx + k, nyx) * Z + z, "rep": r}, device_id_type=MESH,
        ).start()
        return carry

    def wait_all(some, send, recv):
        bulk = pltpu.make_async_remote_copy(
            some, some, send, recv, device_id={"chan": c, "rep": lax.rem(r + 1, reps)}, device_id_type=MESH
        )
        bulk.wait_send()
        bulk.wait_recv()

    lax.fori_loop(1, Z, z_start, 0)
    send_part(1, 1, chans)
    wait_all(srcbuf.at[pl.ds(0, Z - 1)], z_send, z_recv)
    lax.fori_loop(1, nyx, y_start, 0)
    loads[3].wait()
    loads[4].wait()
    def lag_rows(s, carry):
        at = pl.multiple_of(s * LAGS, LAGS)
        for w in range(2):
            u = srcspec[0, pl.ds(w * 32 + s, 1), :]
            v = srcspec[1, pl.ds(w * 32 + s, 1), :]
            cos, sin = lag[0], lag[1]
            lk[w, pl.ds(at, LAGS), 0:256] = (u * cos + v * sin).astype(BF16)
            lk[w, pl.ds(at, LAGS), 256:512] = (v * cos - u * sin).astype(BF16)
        return carry

    near, far = jnp.bitwise_xor(r, 1), jnp.bitwise_xor(r, 2)

    def g_copy(w, k):
        slot = far if k == 2 else r
        return pltpu.make_async_remote_copy(
            gath.at[w, slot], gath.at[w, slot], g_send.at[w, k], g_recv.at[w, k],
            device_id={"chan": c, "rep": far if k == 1 else near}, device_id_type=MESH,
        )

    def own_part(w):
        wait_all(recv.at[w, pl.ds(0, chans - 1)], a_send.at[w], a_recv.at[w])
        re, im = whiten(recv.at[w], dft, absbuf, xbuf, normed)
        mask = jnp.zeros((1, 128), F32)
        for q in range(reps):
            tile = chan_live[w][:, (q // 2) * 128 : (q // 2) * 128 + 128]
            mask = jnp.where(r == q, pltpu.roll(tile, (64 * q) % 128, 1), mask)
        re, im = re * mask, im * mask
        gath[w, r] = jnp.where(iota((K, 128), 1) < 64, re, pltpu.roll(im, 64, 1)).astype(BF16)
        g_copy(w, 1).start()
        g_copy(w, 0).start()

    def forward(w):
        g_copy(w, 1).wait_recv()
        g_copy(w, 2).start()

    def correlate(w):
        g_copy(w, 0).wait_recv()
        g_copy(w, 2).wait_recv()
        for k in range(3):
            g_copy(w, k).wait_send()
        low = iota((K, 128), 1) < 64
        for h in range(2):
            a, b = gath[w, 2 * h], gath[w, 2 * h + 1]
            rhs[0:K, h * 128 : h * 128 + 128] = jnp.where(low, a, swap(b))
            rhs[K:, h * 128 : h * 128 + 128] = jnp.where(low, swap(a), b)

        def rows(i, carry):
            at = pl.multiple_of(i * 256, 256)
            part = jnp.dot(lk[w, pl.ds(at, 256), :], rhs[...], preferred_element_type=F32)
            for k in range(4):
                piece = part[k * LAGS : (k + 1) * LAGS]
                if w == 0:
                    out[i * 4 + k] = piece
                else:
                    out[i * 4 + k] = (out[i * 4 + k] + piece) * inv[pl.ds(i * 4 + k, 1), :]
            return carry

        lax.fori_loop(0, lk.shape[1] // 256, rows, 0)

    own_part(0)
    wait_all(srcbuf.at[pl.ds(0, (nyx - 1) * Z)], y_send, y_recv)
    re, im = whiten(srcbuf, dft, absbuf, xbuf, normed)
    ls_col = jnp.concatenate([ls[0], ls[1]], axis=0)[:, :1]
    for part, value in enumerate((re, im)):
        rows = jnp.transpose(value)[:64] * ls_col
        srcspec[part] = rows.astype(BF16).astype(F32)

    lax.fori_loop(0, 32, lag_rows, 0)

    forward(0)
    own_part(1)
    correlate(0)
    forward(1)
    correlate(1)


def solution(mesh):
    chans, reps = mesh.shape["chan"], mesh.shape["rep"]

    def shards(records, sources, dead_list):
        windows, groups, width, span = records.shape
        length = span * chans
        dft, lag = tables(length)
        quarter = sources.shape[0] // reps
        vmem = pl.BlockSpec(memory_space=pltpu.VMEM)
        hbm = pl.BlockSpec(memory_space=pltpu.HBM)
        dma = pltpu.SemaphoreType.DMA
        return pl.pallas_call(
            functools.partial(gather_kernel, chans, reps),
            out_shape=jax.ShapeDtypeStruct((quarter, LAGS, 256), F32),
            in_specs=[hbm] * 5,
            out_specs=vmem,
            scratch_shapes=[
                pltpu.VMEM((windows, groups, span, width), BF16),
                pltpu.VMEM((1, sources.shape[0]), jnp.int32),
                pltpu.VMEM(dead_list.shape, jnp.int32),
                pltpu.VMEM((512, length), BF16),
                pltpu.VMEM((2, LAGS, K), F32),
                pltpu.VMEM((2, chans, 16, 128), BF16),
                pltpu.VMEM((2, chans, 16, 128), BF16),
                pltpu.VMEM((chans * 16, 256), F32),
                pltpu.VMEM((reps, 16, 128), BF16),
                pltpu.VMEM((reps, 16, 128), BF16),
                pltpu.VMEM((chans, 16, 128), BF16),
                pltpu.VMEM((2, reps, K, 128), BF16),
                pltpu.VMEM((2 * K, 256), BF16),
                pltpu.VMEM((2, quarter * LAGS, 2 * K), BF16),
                pltpu.VMEM((quarter, 256), F32),
                pltpu.VMEM((length // 2 + 128, 128), BF16),
                pltpu.VMEM((length // 2, 128), BF16),
                pltpu.VMEM((length // 2, 128), BF16),
                pltpu.VMEM((2, 64, 256), F32),
                pltpu.VMEM((2, 128, 128), F32),
                dma((5,)), dma((2,)), dma((2,)), dma((reps,)), dma((reps,)),
                dma, dma, dma, dma, dma((2, 3)), dma((2, 3)),
            ],
            compiler_params=pltpu.CompilerParams(
                collective_id=0, has_side_effects=True, vmem_limit_bytes=48 << 20
            ),
            name="correlations",
        )(
            *[
                pltpu.with_memory_space_constraint(x, pltpu.HBM)
                for x in (
                    jnp.transpose(records, (0, 1, 3, 2)),
                    sources.reshape(1, -1),
                    dead_list,
                    jnp.asarray(dft),
                    jnp.asarray(lag),
                )
            ]
        )

    return jax.shard_map(
        shards,
        mesh=mesh,
        in_specs=(P(None, None, "rep", "chan"), P(), P()),
        out_specs=P("rep", None, "chan"),
        check_vma=False,
    )
```

time: 72.3 us -> 41.5 us (0.57)
  Pallas kernels: 62.7 us -> 40.1 us
  local copies, waits for them, and re-layouts: 9.12 us -> 1.32 us
    pallas_call x2 -> x1, Pallas kernels: 62.7 us -> 40.1 us  [shards(): pl.pallas_call(functools.partial(gather_kernel, chans, reps), out_shape=j...]
    unnamed x20 -> x1, local copies, waits for them, and re-layouts: 9.12 us -> 1.32 us
where the time goes in v2:
time: 41.5 us; the launch traced here: 41.4 us
  Pallas kernels  40.1 us (97%)
  local copies, waits for them, and re-layouts  1.32 us (3%)
    pallas_call x1, Pallas kernels, shards(): pl.pallas_call(functools.partial(gather_kernel, chans, reps), out_shape=j...  40.1 us
    unnamed x1, local copies, waits for them, and re-layouts  1.32 us

profile of v2, /device:TPU:1, one launch (start us, length us, event | category | flops | bytes accessed | tf_op | source)
XLA Modules:
  0.0 41.4 jit_solution(233103234473531682)
XLA Ops:
  0.0 40.1 %correlations.1 = f32[32,64,256]{2,1,0:T(8,128)S(1)} custom-call(bf16[2,64,32,64]{3,2,1,0:T(8,128)(2,1)} %bitcast.2, s32[1,128]{1,0:T(1,128)} %bitcast.3, s32[2,1024]{1,0:T(2,128)} %dead_hbm.1, bf16[512,2048]{1,0:T(8,128)(2,1)} %constant.4.clone.dft_hbm, f32[2,64,256]{2,1,0:T(8,128)} %constant.5.clone.lag_hbm), custom_call_target="tpu_custom_call" | custom-call | tf_op jit(solution)/shard_map/correlations/pallas_call | solution.py:334
  40.1 1.3 %copy.7 = f32[32,64,256]{2,1,0:T(8,128)} copy(f32[32,64,256]{2,1,0:T(8,128)S(1)} %correlations.1) | data formatting | bytes 4194304

commit v3 on v2

--- a/solution.py
+++ b/solution.py
@@ -105,11 +105,14 @@
     loads = [
         pltpu.make_async_copy(a, b, sem_in.at[i])
         for i, (a, b) in enumerate(
-            [(rec_hbm, rec), (src_hbm, src_ref), (dead_hbm, dead_ref), (dft_hbm, dft), (lag_hbm, lag)]
+            [
+                (rec_hbm.at[0], rec.at[0]), (src_hbm, src_ref), (dead_hbm, dead_ref), (dft_hbm, dft), (lag_hbm, lag),
+                (rec_hbm.at[1], rec.at[1]),
+            ]
         )
     ]
-    for load in loads:
-        load.start()
+    for i in (0, 5, 1, 2, 3, 4):
+        loads[i].start()
 
     def greet(k, carry):
         pl.semaphore_signal(barrier, inc=1, device_id={"chan": lax.rem(c + k, chans), "rep": r}, device_id_type=MESH)
@@ -121,18 +124,20 @@
 
     loads[0].wait()
 
-    def pack(i, carry):
-        for k in range(8):
-            g = i * 8 + k
-            for w in range(2):
+    def pack_window(w):
+        def pack(i, carry):
+            for k in range(8):
+                g = i * 8 + k
                 packed[w, g] = jnp.concatenate([rec[w, g, 0:16], rec[w, g, 16:32]], axis=1)
-        return carry
-
-    lax.fori_loop(0, chans // 8, pack, 0)
-    for w in range(2):
+            return carry
+
+        lax.fori_loop(0, chans // 8, pack, 0)
         recv[w, c] = packed[w, c]
 
+    pack_window(0)
     pl.semaphore_wait(barrier, chans - 1 + reps - 1)
+
+    some_zero, some_one = chans * 3 // 8, chans * 5 // 8
 
     def send_part(w, first, last):
         def send(k, carry):
@@ -145,7 +150,9 @@
 
         lax.fori_loop(first, last, send, 0)
 
-    send_part(0, 1, chans)
+    send_part(0, 1, some_zero)
+    loads[5].wait()
+    pack_window(1)
 
     loads[1].wait()
     src = src_ref[...]
@@ -186,6 +193,7 @@
 
     for k in range(1, reps):
         p_copy(k).start()
+    send_part(0, some_zero, chans)
 
     loads[2].wait()
     dead = dead_ref[...]
@@ -239,9 +247,10 @@
         bulk.wait_recv()
 
     lax.fori_loop(1, Z, z_start, 0)
-    send_part(1, 1, chans)
+    send_part(1, 1, some_one)
     wait_all(srcbuf.at[pl.ds(0, Z - 1)], z_send, z_recv)
     lax.fori_loop(1, nyx, y_start, 0)
+    send_part(1, some_one, chans)
     loads[3].wait()
     loads[4].wait()
     def lag_rows(s, carry):
@@ -254,13 +263,10 @@
             lk[w, pl.ds(at, LAGS), 256:512] = (v * cos - u * sin).astype(BF16)
         return carry
 
-    near, far = jnp.bitwise_xor(r, 1), jnp.bitwise_xor(r, 2)
-
     def g_copy(w, k):
-        slot = far if k == 2 else r
         return pltpu.make_async_remote_copy(
-            gath.at[w, slot], gath.at[w, slot], g_send.at[w, k], g_recv.at[w, k],
-            device_id={"chan": c, "rep": far if k == 1 else near}, device_id_type=MESH,
+            gath.at[w, r], gath.at[w, r], g_send.at[w, k], g_recv.at[w, k],
+            device_id={"chan": c, "rep": jnp.bitwise_xor(r, k)}, device_id_type=MESH,
         )
 
     def own_part(w):
@@ -272,17 +278,12 @@
             mask = jnp.where(r == q, pltpu.roll(tile, (64 * q) % 128, 1), mask)
         re, im = re * mask, im * mask
         gath[w, r] = jnp.where(iota((K, 128), 1) < 64, re, pltpu.roll(im, 64, 1)).astype(BF16)
-        g_copy(w, 1).start()
-        g_copy(w, 0).start()
-
-    def forward(w):
-        g_copy(w, 1).wait_recv()
-        g_copy(w, 2).start()
+        for k in (2, 3, 1):
+            g_copy(w, k).start()
 
     def correlate(w):
-        g_copy(w, 0).wait_recv()
-        g_copy(w, 2).wait_recv()
-        for k in range(3):
+        for k in range(1, reps):
+            g_copy(w, k).wait_recv()
             g_copy(w, k).wait_send()
         low = iota((K, 128), 1) < 64
         for h in range(2):
@@ -290,18 +291,13 @@
             rhs[0:K, h * 128 : h * 128 + 128] = jnp.where(low, a, swap(b))
             rhs[K:, h * 128 : h * 128 + 128] = jnp.where(low, swap(a), b)
 
-        def rows(i, carry):
-            at = pl.multiple_of(i * 256, 256)
-            part = jnp.dot(lk[w, pl.ds(at, 256), :], rhs[...], preferred_element_type=F32)
-            for k in range(4):
-                piece = part[k * LAGS : (k + 1) * LAGS]
-                if w == 0:
-                    out[i * 4 + k] = piece
-                else:
-                    out[i * 4 + k] = (out[i * 4 + k] + piece) * inv[pl.ds(i * 4 + k, 1), :]
-            return carry
-
-        lax.fori_loop(0, lk.shape[1] // 256, rows, 0)
+        part = jnp.dot(lk[w], rhs[...], preferred_element_type=F32)
+        for k in range(out.shape[0]):
+            piece = part[k * LAGS : (k + 1) * LAGS]
+            if w == 0:
+                out[k] = piece
+            else:
+                out[k] = (out[k] + piece) * inv[k : k + 1, :]
 
     own_part(0)
     wait_all(srcbuf.at[pl.ds(0, (nyx - 1) * Z)], y_send, y_recv)
@@ -313,10 +309,8 @@
 
     lax.fori_loop(0, 32, lag_rows, 0)
 
-    forward(0)
     own_part(1)
     correlate(0)
-    forward(1)
     correlate(1)
 
 
@@ -357,8 +351,8 @@
                 pltpu.VMEM((length // 2, 128), BF16),
                 pltpu.VMEM((2, 64, 256), F32),
                 pltpu.VMEM((2, 128, 128), F32),
-                dma((5,)), dma((2,)), dma((2,)), dma((reps,)), dma((reps,)),
-                dma, dma, dma, dma, dma((2, 3)), dma((2, 3)),
+                dma((6,)), dma((2,)), dma((2,)), dma((reps,)), dma((reps,)),
+                dma, dma, dma, dma, dma((2, reps)), dma((2, reps)),
             ],
             compiler_params=pltpu.CompilerParams(
                 collective_id=0, has_side_effects=True, vmem_limit_bytes=48 << 20

time: 41.5 us -> 40.4 us (0.973)
  Pallas kernels: 40.1 us -> 39 us
    pallas_call x1, Pallas kernels: 40.1 us -> 39 us  [shards(): pl.pallas_call(functools.partial(gather_kernel, chans, reps), out_shape=j...]
where the time goes in v3:
time: 40.4 us; the launch traced here: 40.3 us
  Pallas kernels  39 us (97%)
  local copies, waits for them, and re-layouts  1.32 us (3%)
    pallas_call x1, Pallas kernels, shards(): pl.pallas_call(functools.partial(gather_kernel, chans, reps), out_shape=j...  39 us
    unnamed x1, local copies, waits for them, and re-layouts  1.32 us

profile of v3, /device:TPU:1, one launch (start us, length us, event | category | flops | bytes accessed | tf_op | source)
XLA Modules:
  0.0 40.3 jit_solution(2715240339849277798)
XLA Ops:
  0.0 39.0 %correlations.1 = f32[32,64,256]{2,1,0:T(8,128)S(1)} custom-call(bf16[2,64,32,64]{3,2,1,0:T(8,128)(2,1)} %bitcast.2, s32[1,128]{1,0:T(1,128)} %bitcast.3, s32[2,1024]{1,0:T(2,128)} %dead_hbm.1, bf16[512,2048]{1,0:T(8,128)(2,1)} %constant.4.clone.dft_hbm, f32[2,64,256]{2,1,0:T(8,128)} %constant.5.clone.lag_hbm), custom_call_target="tpu_custom_call" | custom-call | tf_op jit(solution)/shard_map/correlations/pallas_call | solution.py:328
  39.0 1.3 %copy.7 = f32[32,64,256]{2,1,0:T(8,128)} copy(f32[32,64,256]{2,1,0:T(8,128)S(1)} %correlations.1) | data formatting | bytes 4194304

commit v4 on v3

--- a/solution.py
+++ b/solution.py
@@ -92,9 +92,9 @@
 def gather_kernel(
     chans, reps,
     rec_hbm, src_hbm, dead_hbm, dft_hbm, lag_hbm,
-    out,
+    out, lk1, rhs, inv,
     rec, src_ref, dead_ref, dft, lag,
-    packed, recv, cols, picks, pickrecv, srcbuf, gath, rhs, lk, inv, absbuf, xbuf, normed, srcspec, livesrc,
+    packed, recv, cols, picks, pickrecv, srcbuf, gath, rhs0, lk0, absbuf, xbuf, normed, srcspec, livesrc,
     sem_in, a_send, a_recv, p_send, p_recv, z_send, z_recv, y_send, y_recv, g_send, g_recv,
 ):
     c, r = lax.axis_index("chan"), lax.axis_index("rep")
@@ -259,8 +259,9 @@
             u = srcspec[0, pl.ds(w * 32 + s, 1), :]
             v = srcspec[1, pl.ds(w * 32 + s, 1), :]
             cos, sin = lag[0], lag[1]
-            lk[w, pl.ds(at, LAGS), 0:256] = (u * cos + v * sin).astype(BF16)
-            lk[w, pl.ds(at, LAGS), 256:512] = (v * cos - u * sin).astype(BF16)
+            lk = lk1 if w else lk0
+            lk[pl.ds(at, LAGS), 0:256] = (u * cos + v * sin).astype(BF16)
+            lk[pl.ds(at, LAGS), 256:512] = (v * cos - u * sin).astype(BF16)
         return carry
 
     def g_copy(w, k):
@@ -286,18 +287,15 @@
             g_copy(w, k).wait_recv()
             g_copy(w, k).wait_send()
         low = iota((K, 128), 1) < 64
+        to = rhs if w else rhs0
         for h in range(2):
             a, b = gath[w, 2 * h], gath[w, 2 * h + 1]
-            rhs[0:K, h * 128 : h * 128 + 128] = jnp.where(low, a, swap(b))
-            rhs[K:, h * 128 : h * 128 + 128] = jnp.where(low, swap(a), b)
-
-        part = jnp.dot(lk[w], rhs[...], preferred_element_type=F32)
-        for k in range(out.shape[0]):
-            piece = part[k * LAGS : (k + 1) * LAGS]
-            if w == 0:
-                out[k] = piece
-            else:
-                out[k] = (out[k] + piece) * inv[k : k + 1, :]
+            to[0:K, h * 128 : h * 128 + 128] = jnp.where(low, a, swap(b))
+            to[K:, h * 128 : h * 128 + 128] = jnp.where(low, swap(a), b)
+        if w == 0:
+            part = jnp.dot(lk0[...], rhs0[...], preferred_element_type=F32)
+            for k in range(out.shape[0]):
+                out[k] = part[k * LAGS : (k + 1) * LAGS]
 
     own_part(0)
     wait_all(srcbuf.at[pl.ds(0, (nyx - 1) * Z)], y_send, y_recv)
@@ -312,6 +310,15 @@
     own_part(1)
     correlate(0)
     correlate(1)
+
+
+def correlate_kernel(part, lk, rhs, inv, out):
+    count = out.shape[0]
+    first = pl.program_id(0) * count
+    rows = pl.ds(pl.multiple_of(first * LAGS, count * LAGS), count * LAGS)
+    summed = jnp.dot(lk[rows, :], rhs[...], preferred_element_type=F32)
+    for k in range(count):
+        out[k] = (part[first + k] + summed[k * LAGS : (k + 1) * LAGS]) * inv[pl.ds(first + k, 1), :]
 
 
 def solution(mesh):
@@ -325,11 +332,16 @@
         vmem = pl.BlockSpec(memory_space=pltpu.VMEM)
         hbm = pl.BlockSpec(memory_space=pltpu.HBM)
         dma = pltpu.SemaphoreType.DMA
-        return pl.pallas_call(
+        partial = pl.pallas_call(
             functools.partial(gather_kernel, chans, reps),
-            out_shape=jax.ShapeDtypeStruct((quarter, LAGS, 256), F32),
+            out_shape=[
+                jax.ShapeDtypeStruct((quarter, LAGS, 256), F32),
+                jax.ShapeDtypeStruct((quarter * LAGS, 2 * K), BF16),
+                jax.ShapeDtypeStruct((2 * K, 256), BF16),
+                jax.ShapeDtypeStruct((quarter, 256), F32),
+            ],
             in_specs=[hbm] * 5,
-            out_specs=vmem,
+            out_specs=[vmem] * 4,
             scratch_shapes=[
                 pltpu.VMEM((windows, groups, span, width), BF16),
                 pltpu.VMEM((1, sources.shape[0]), jnp.int32),
@@ -344,8 +356,7 @@
                 pltpu.VMEM((chans, 16, 128), BF16),
                 pltpu.VMEM((2, reps, K, 128), BF16),
                 pltpu.VMEM((2 * K, 256), BF16),
-                pltpu.VMEM((2, quarter * LAGS, 2 * K), BF16),
-                pltpu.VMEM((quarter, 256), F32),
+                pltpu.VMEM((quarter * LAGS, 2 * K), BF16),
                 pltpu.VMEM((length // 2 + 128, 128), BF16),
                 pltpu.VMEM((length // 2, 128), BF16),
                 pltpu.VMEM((length // 2, 128), BF16),
@@ -370,6 +381,16 @@
                 )
             ]
         )
+        step = 16
+        return pl.pallas_call(
+            correlate_kernel,
+            grid=(quarter // step,),
+            out_shape=jax.ShapeDtypeStruct((quarter, LAGS, 256), F32),
+            in_specs=[vmem] * 4,
+            out_specs=pl.BlockSpec((step, LAGS, 256), lambda i: (i, 0, 0)),
+            compiler_params=pltpu.CompilerParams(vmem_limit_bytes=16 << 20),
+            name="correlate",
+        )(*partial)
 
     return jax.shard_map(
         shards,

time: 40.4 us -> 39.7 us (0.983)
  local copies, waits for them, and re-layouts: 1.32 us -> 0 us
  Pallas kernels: 39 us -> 39.7 us
    unnamed x1 -> x0, local copies, waits for them, and re-layouts: 1.32 us -> none
    pallas_call x1 -> x2, Pallas kernels: 39 us -> 39.7 us  [the longest x1 37.8 us: shards(): pl.pallas_call(functools.partial(gather_kernel, chans, reps), out_shape=[...]
where the time goes in v4:
time: 39.7 us
  Pallas kernels  39.7 us (100%)
    pallas_call x1, Pallas kernels, shards(): pl.pallas_call(functools.partial(gather_kernel, chans, reps), out_shape=[...  37.8 us
    pallas_call x1, Pallas kernels, shards(): pl.pallas_call(correlate_kernel, grid=(quarter // step,), out_shape=jax.S...  1.87 us

profile of v4, /device:TPU:1, one launch (start us, length us, event | category | flops | bytes accessed | tf_op | source)
XLA Modules:
  0.0 39.7 jit_solution(2102912986440436767)
XLA Ops:
  0.0 37.8 %correlations.1 = (f32[32,64,256]{2,1,0:T(8,128)S(1)}, bf16[2048,512]{1,0:T(8,128)(2,1)S(1)}, bf16[512,256]{1,0:T(8,128)(2,1)S(1)}, f32[32,256]{1,0:T(8,128)S(1)}) custom-call(bf16[2,64,32,64]{3,2,1,0:T(8,128)(2,1)} %bitcast.2, s32[1,128]{1,0:T(1,128)} %bitcast.3, s32[2,1024]{1,0:T(2,128)} %dead_hbm.1, bf16[512,2048]{1,0:T(8,128)(2,1)} %constant.4.clone.dft_hbm, ...), custom_call_target="tpu_custom_call" | custom-call | tf_op jit(solution)/shard_map/correlations/pallas_call | solution.py:335
  37.8 1.9 %correlate.1 = f32[32,64,256]{2,1,0:T(8,128)} custom-call(f32[32,64,256]{2,1,0:T(8,128)S(1)} %get-tuple-element.9.part, bf16[2048,512]{1,0:T(8,128)(2,1)S(1)} %get-tuple-element.10.lk, bf16[512,256]{1,0:T(8,128)(2,1)S(1)} %get-tuple-element.11.rhs, f32[32,256]{1,0:T(8,128)S(1)} %get-tuple-element.12.inv), custom_call_target="tpu_custom_call" | custom-call | tf_op jit(solution)/shard_map/correlate/pallas_call | solution.py:385

commit v5 on v4

--- a/solution.py
+++ b/solution.py
@@ -239,11 +239,13 @@
         ).start()
         return carry
 
+    sent = []
+
     def wait_all(some, send, recv):
         bulk = pltpu.make_async_remote_copy(
             some, some, send, recv, device_id={"chan": c, "rep": lax.rem(r + 1, reps)}, device_id_type=MESH
         )
-        bulk.wait_send()
+        sent.append(bulk)
         bulk.wait_recv()
 
     lax.fori_loop(1, Z, z_start, 0)
@@ -285,7 +287,7 @@
     def correlate(w):
         for k in range(1, reps):
             g_copy(w, k).wait_recv()
-            g_copy(w, k).wait_send()
+            sent.append(g_copy(w, k))
         low = iota((K, 128), 1) < 64
         to = rhs if w else rhs0
         for h in range(2):
@@ -298,6 +300,7 @@
                 out[k] = part[k * LAGS : (k + 1) * LAGS]
 
     own_part(0)
+    own_part(1)
     wait_all(srcbuf.at[pl.ds(0, (nyx - 1) * Z)], y_send, y_recv)
     re, im = whiten(srcbuf, dft, absbuf, xbuf, normed)
     ls_col = jnp.concatenate([ls[0], ls[1]], axis=0)[:, :1]
@@ -307,18 +310,25 @@
 
     lax.fori_loop(0, 32, lag_rows, 0)
 
-    own_part(1)
     correlate(0)
     correlate(1)
-
-
-def correlate_kernel(part, lk, rhs, inv, out):
-    count = out.shape[0]
-    first = pl.program_id(0) * count
-    rows = pl.ds(pl.multiple_of(first * LAGS, count * LAGS), count * LAGS)
-    summed = jnp.dot(lk[rows, :], rhs[...], preferred_element_type=F32)
-    for k in range(count):
-        out[k] = (part[first + k] + summed[k * LAGS : (k + 1) * LAGS]) * inv[pl.ds(first + k, 1), :]
+    for bulk in sent:
+        bulk.wait_send()
+
+
+def correlate_kernel(part, lk, rhs, inv, out, buf, sem):
+    parts = sem.shape[0]
+    count = out.shape[0] // parts
+    copies = []
+    for p in range(parts):
+        first = p * count
+        summed = jnp.dot(lk[first * LAGS : (first + count) * LAGS, :], rhs[...], preferred_element_type=F32)
+        for k in range(count):
+            buf[first + k] = (part[first + k] + summed[k * LAGS : (k + 1) * LAGS]) * inv[first + k : first + k + 1, :]
+        copies.append(pltpu.make_async_copy(buf.at[pl.ds(first, count)], out.at[pl.ds(first, count)], sem.at[p]))
+        copies[-1].start()
+    for copy in copies:
+        copy.wait()
 
 
 def solution(mesh):
@@ -381,13 +391,12 @@
                 )
             ]
         )
-        step = 16
         return pl.pallas_call(
             correlate_kernel,
-            grid=(quarter // step,),
             out_shape=jax.ShapeDtypeStruct((quarter, LAGS, 256), F32),
             in_specs=[vmem] * 4,
-            out_specs=pl.BlockSpec((step, LAGS, 256), lambda i: (i, 0, 0)),
+            out_specs=hbm,
+            scratch_shapes=[pltpu.VMEM((quarter, LAGS, 256), F32), dma((4,))],
             compiler_params=pltpu.CompilerParams(vmem_limit_bytes=16 << 20),
             name="correlate",
         )(*partial)

time: 39.7 us -> 37.3 us (0.940)
  Pallas kernels: 39.7 us -> 37.3 us
    pallas_call x1, Pallas kernels: 37.8 us -> 35.5 us  [shards(): pl.pallas_call(functools.partial(gather_kernel, chans, reps), out_shape=[...]
where the time goes in v5:
time: 37.3 us
  Pallas kernels  37.3 us (100%)
    pallas_call x1, Pallas kernels, shards(): pl.pallas_call(functools.partial(gather_kernel, chans, reps), out_shape=[...  35.5 us
    pallas_call x1, Pallas kernels, shards(): pl.pallas_call(correlate_kernel, out_shape=jax.ShapeDtypeStruct((quarter,...  1.8 us

profile of v5, /device:TPU:1, one launch (start us, length us, event | category | flops | bytes accessed | tf_op | source)
XLA Modules:
  0.0 37.3 jit_solution(11419445184155781123)
XLA Ops:
  0.0 35.5 %correlations.1 = (f32[32,64,256]{2,1,0:T(8,128)S(1)}, bf16[2048,512]{1,0:T(8,128)(2,1)S(1)}, bf16[512,256]{1,0:T(8,128)(2,1)S(1)}, f32[32,256]{1,0:T(8,128)S(1)}) custom-call(bf16[2,64,32,64]{3,2,1,0:T(8,128)(2,1)} %bitcast.2, s32[1,128]{1,0:T(1,128)} %bitcast.3, s32[2,1024]{1,0:T(2,128)} %dead_hbm.1, bf16[512,2048]{1,0:T(8,128)(2,1)} %constant.4.clone.dft_hbm, ...), custom_call_target="tpu_custom_call" | custom-call | tf_op jit(solution)/shard_map/correlations/pallas_call | solution.py:345
  35.5 1.8 %correlate.1 = f32[32,64,256]{2,1,0:T(8,128)} custom-call(f32[32,64,256]{2,1,0:T(8,128)S(1)} %get-tuple-element.9.part, bf16[2048,512]{1,0:T(8,128)(2,1)S(1)} %get-tuple-element.10.lk, bf16[512,256]{1,0:T(8,128)(2,1)S(1)} %get-tuple-element.11.rhs, f32[32,256]{1,0:T(8,128)S(1)} %get-tuple-element.12.inv), custom_call_target="tpu_custom_call" | custom-call | tf_op jit(solution)/shard_map/correlate/pallas_call | solution.py:394

commit v6 on v5

--- a/solution.py
+++ b/solution.py
@@ -137,7 +137,7 @@
     pack_window(0)
     pl.semaphore_wait(barrier, chans - 1 + reps - 1)
 
-    some_zero, some_one = chans * 3 // 8, chans * 5 // 8
+    some_zero = chans * 3 // 8
 
     def send_part(w, first, last):
         def send(k, carry):
@@ -249,10 +249,9 @@
         bulk.wait_recv()
 
     lax.fori_loop(1, Z, z_start, 0)
-    send_part(1, 1, some_one)
+    send_part(1, 1, chans)
     wait_all(srcbuf.at[pl.ds(0, Z - 1)], z_send, z_recv)
     lax.fori_loop(1, nyx, y_start, 0)
-    send_part(1, some_one, chans)
     loads[3].wait()
     loads[4].wait()
     def lag_rows(s, carry):

time: 37.3 us -> 35.9 us (0.962)
  Pallas kernels: 37.3 us -> 35.8 us
    pallas_call x1, Pallas kernels: 35.5 us -> 34 us  [shards(): pl.pallas_call(functools.partial(gather_kernel, chans, reps), out_shape=[...]
where the time goes in v6:
time: 35.9 us
  Pallas kernels  35.8 us (100%)
    pallas_call x1, Pallas kernels, shards(): pl.pallas_call(functools.partial(gather_kernel, chans, reps), out_shape=[...  34 us
    pallas_call x1, Pallas kernels, shards(): pl.pallas_call(correlate_kernel, out_shape=jax.ShapeDtypeStruct((quarter,...  1.8 us

profile of v6, /device:TPU:1, one launch (start us, length us, event | category | flops | bytes accessed | tf_op | source)
XLA Modules:
  0.0 35.9 jit_solution(16988026717819383174)
XLA Ops:
  0.0 34.0 %correlations.1 = (f32[32,64,256]{2,1,0:T(8,128)S(1)}, bf16[2048,512]{1,0:T(8,128)(2,1)S(1)}, bf16[512,256]{1,0:T(8,128)(2,1)S(1)}, f32[32,256]{1,0:T(8,128)S(1)}) custom-call(bf16[2,64,32,64]{3,2,1,0:T(8,128)(2,1)} %bitcast.2, s32[1,128]{1,0:T(1,128)} %bitcast.3, s32[2,1024]{1,0:T(2,128)} %dead_hbm.1, bf16[512,2048]{1,0:T(8,128)(2,1)} %constant.4.clone.dft_hbm, ...), custom_call_target="tpu_custom_call" | custom-call | tf_op jit(solution)/shard_map/correlations/pallas_call | solution.py:344
  34.1 1.8 %correlate.1 = f32[32,64,256]{2,1,0:T(8,128)} custom-call(f32[32,64,256]{2,1,0:T(8,128)S(1)} %get-tuple-element.9.part, bf16[2048,512]{1,0:T(8,128)(2,1)S(1)} %get-tuple-element.10.lk, bf16[512,256]{1,0:T(8,128)(2,1)S(1)} %get-tuple-element.11.rhs, f32[32,256]{1,0:T(8,128)S(1)} %get-tuple-element.12.inv), custom_call_target="tpu_custom_call" | custom-call | tf_op jit(solution)/shard_map/correlate/pallas_call | solution.py:393

commit v7 on v6

--- a/solution.py
+++ b/solution.py
@@ -195,6 +195,8 @@
         p_copy(k).start()
     send_part(0, some_zero, chans)
 
+    send_part(1, 1, chans)
+
     loads[2].wait()
     dead = dead_ref[...]
     eye = iota((128, 128), 0) == iota((128, 128), 1)
@@ -249,7 +251,6 @@
         bulk.wait_recv()
 
     lax.fori_loop(1, Z, z_start, 0)
-    send_part(1, 1, chans)
     wait_all(srcbuf.at[pl.ds(0, Z - 1)], z_send, z_recv)
     lax.fori_loop(1, nyx, y_start, 0)
     loads[3].wait()

time: 35.9 us -> 39.6 us (1.10)
  Pallas kernels: 35.8 us -> 39.5 us
    pallas_call x1, Pallas kernels: 34 us -> 37.7 us  [shards(): pl.pallas_call(functools.partial(gather_kernel, chans, reps), out_shape=[...]
where the time goes in v7:
time: 39.6 us; the launch traced here: 39.5 us
  Pallas kernels  39.5 us (100%)
    pallas_call x1, Pallas kernels, shards(): pl.pallas_call(functools.partial(gather_kernel, chans, reps), out_shape=[...  37.7 us
    pallas_call x1, Pallas kernels, shards(): pl.pallas_call(correlate_kernel, out_shape=jax.ShapeDtypeStruct((quarter,...  1.8 us

profile of v7, /device:TPU:1, one launch (start us, length us, event | category | flops | bytes accessed | tf_op | source)
XLA Modules:
  0.0 39.5 jit_solution(15607293450040128160)
XLA Ops:
  0.0 37.7 %correlations.1 = (f32[32,64,256]{2,1,0:T(8,128)S(1)}, bf16[2048,512]{1,0:T(8,128)(2,1)S(1)}, bf16[512,256]{1,0:T(8,128)(2,1)S(1)}, f32[32,256]{1,0:T(8,128)S(1)}) custom-call(bf16[2,64,32,64]{3,2,1,0:T(8,128)(2,1)} %bitcast.2, s32[1,128]{1,0:T(1,128)} %bitcast.3, s32[2,1024]{1,0:T(2,128)} %dead_hbm.1, bf16[512,2048]{1,0:T(8,128)(2,1)} %constant.4.clone.dft_hbm, ...), custom_call_target="tpu_custom_call" | custom-call | tf_op jit(solution)/shard_map/correlations/pallas_call | solution.py:345
  37.7 1.8 %correlate.1 = f32[32,64,256]{2,1,0:T(8,128)} custom-call(f32[32,64,256]{2,1,0:T(8,128)S(1)} %get-tuple-element.9.part, bf16[2048,512]{1,0:T(8,128)(2,1)S(1)} %get-tuple-element.10.lk, bf16[512,256]{1,0:T(8,128)(2,1)S(1)} %get-tuple-element.11.rhs, f32[32,256]{1,0:T(8,128)S(1)} %get-tuple-element.12.inv), custom_call_target="tpu_custom_call" | custom-call | tf_op jit(solution)/shard_map/correlate/pallas_call | solution.py:394
